TPU v7x, 256 devices: a whole 4x4x8 slice. The times are simulated.
256 devices in a mesh: chan: 64 (over y, z, core), hour: 4 (over x).
Axes of the slice: x: 4, y: 4, z: 8, core: 2. Of those that a mesh axis runs over, the one named last changes fastest.
Arguments:
- spectra: bfloat16 [8, 2, 8192, 2560], P('hour', None, 'chan'), may hold values from -34 to 34, as said below
- partner_lists: int32 [64, 4], replicated, may hold values from -1 to 63, as said below
- partner_counts: int32 [64], replicated, may hold values from 2 to 4, as said below
Outputs:
- stacks: float32 [256, 8, 128, 256], P(('chan', 'hour'))
Inputs may be any that keep to these rules, and one draw needn't show every extreme that they name: The spectra are finite and bounded. `partner_lists`: row s lists distinct channel blocks, the first being s itself; entries from position partner_counts[s] on are -1. Within their counts, every block is listed by at most 4 rows, and some block by exactly 4. `partner_counts`: some row has exactly 4 partners.
All inputs are finite; a program needn't handle non-finite values.
Results may differ from a plain program's by a relative error of at most 0.0046.
Values may be sent and summed in bfloat16 or wider, within the bound.
A program may use at most 128 MiB of HBM per device.

v0:
```python
import math
import jax
import jax.numpy as jnp
from jax import lax
from jax.sharding import PartitionSpec as P

VS = 8
F0 = 64
NWIN = 8192
SMOOTH = 129
LAGS = 256


def whiten(real_part, imag_part):
    amplitude = jnp.sqrt(real_part * real_part + imag_part * imag_part)
    window_shape = (1,) * (amplitude.ndim - 1) + (SMOOTH,)
    padding = ((0, 0),) * (amplitude.ndim - 1) + ((SMOOTH // 2, SMOOTH // 2),)
    summed = lax.reduce_window(
        amplitude,
        jnp.zeros((), amplitude.dtype),
        lax.add,
        window_shape,
        (1,) * amplitude.ndim,
        padding,
    )
    denominator = summed / SMOOTH + 1e-06
    return (
        (real_part / denominator).astype(jnp.bfloat16),
        (imag_part / denominator).astype(jnp.bfloat16),
    )


def lag_table(band_bins):
    freq_index = jnp.arange(band_bins, dtype=jnp.int32)[:, None] + F0
    lag_index = jnp.arange(LAGS, dtype=jnp.int32)[None, :] - LAGS // 2
    lag_index = jnp.where(lag_index < 0, lag_index + NWIN, lag_index)
    phase_index = freq_index * lag_index % NWIN
    phase_angle = phase_index.astype(jnp.float32) * (2.0 * math.pi / NWIN)
    return jnp.concatenate([jnp.cos(phase_angle), -jnp.sin(phase_angle)], 0).astype(jnp.bfloat16)


def slot_onehot(partner_lists, partner_counts, receiver):
    offsets = jnp.arange(partner_lists.shape[1], dtype=jnp.int32)
    listed = (offsets[None, :] < partner_counts[:, None]) & (partner_lists == receiver)
    member = jnp.any(listed, axis=1)
    slot_rank = jnp.cumsum(member.astype(jnp.int32)) - 1
    slots = jnp.arange(partner_lists.shape[1], dtype=jnp.int32)
    return member[None, :] & (slot_rank[None, :] == slots[:, None])


def shards(spectra, partner_lists, partner_counts):
    windows, _, block_chans, band_bins = spectra.shape
    block_count = lax.axis_size("chan")
    hour_count = lax.axis_size("hour")
    values = spectra.astype(jnp.float32)
    white_re, white_im = whiten(values[:, 0], values[:, 1])
    stride = block_chans // VS
    local_sources = jnp.stack([white_re[:, ::stride, :], white_im[:, ::stride, :]], 1)
    local_sources = jnp.transpose(local_sources, (2, 0, 1, 3))
    receiver = lax.axis_index("chan")
    onehot = slot_onehot(partner_lists, partner_counts, receiver).astype(jnp.bfloat16)
    slot_total = onehot.shape[0]
    gathered = lax.all_gather(local_sources, "chan", axis=0, tiled=True)
    flattened = gathered.reshape(block_count, -1)
    chosen = jnp.dot(onehot, flattened, preferred_element_type=jnp.float32)
    chosen = chosen.reshape(slot_total, VS, windows, 2, band_bins)
    table_values = lag_table(band_bins)
    norm_scale = 1.0 / math.sqrt(4.0 * band_bins * windows * hour_count)

    def one_slot(source):
        cross_re = jnp.zeros((VS, block_chans, band_bins), jnp.float32)
        cross_im = jnp.zeros((VS, block_chans, band_bins), jnp.float32)
        for window in range(windows):
            src_real = source[:, window, 0][:, None, :]
            src_imag = source[:, window, 1][:, None, :]
            recv_real = white_re[window][None, :, :]
            recv_imag = white_im[window][None, :, :]
            cross_re = cross_re + src_real * recv_real + src_imag * recv_imag
            cross_im = cross_im + src_imag * recv_real - src_real * recv_imag
        cross = (
            jnp.concatenate([cross_re, cross_im], -1)
            .astype(jnp.bfloat16)
            .reshape(VS * block_chans, 2 * band_bins)
        )
        lagged = jnp.dot(cross, table_values, preferred_element_type=jnp.float32) * norm_scale
        return lagged.reshape(VS, block_chans, LAGS)

    partial_stacks = lax.map(one_slot, chosen)
    summed_hours = lax.psum(partial_stacks, "hour")
    share = slot_total // hour_count
    return lax.dynamic_slice_in_dim(summed_hours, lax.axis_index("hour") * share, share, 0)


def solution(mesh):
    return jax.shard_map(
        shards,
        mesh=mesh,
        in_specs=(P("hour", None, "chan", None), P(), P()),
        out_specs=P(("chan", "hour"), None, None, None),
        check_vma=False,
    )
```

profile of v0, /device:TPU:1, one launch (start us, length us, event | category | flops | bytes accessed | tf_op | source)
XLA Modules:
  0.0 464.1 jit_solution(17760751546049418316)
XLA Ops:
  6.5 0.0 all-gather.2.cloned.1.call-start
  6.5 3.2 copy.26
  9.8 0.3 convert_element_type.43
  10.1 0.0 copy-start
  10.1 2.3 copy-done
  12.4 0.8 add_sqrt_fusion
  13.3 129.2 %reduce_window.7 = f32[2,128,2560]{1,2,0:T(8,128)} reduce-window(f32[2,128,2560]{1,2,0:T(8,128)S(1)} %add_sqrt_fusion, f32[]{:T(128)} %constant.29.clone.1), window={size=1x1x129 pad=0_0x0_0x64_64}, to_apply=%region_2.0 | reduce-window | flops 83886080 | bytes 5242884 | tf_op jit(solution)/shard_map/reduce_window | solution.py:18
  142.4 4.0 divide_convert_fusion.1
  146.4 0.0 copy-start.1
  146.4 10.4 %slice.38 = bf16[2,8,2560]{1,2,0:T(8,128)(2,1)} slice(bf16[2,128,2560]{1,2,0:T(8,128)(2,1)S(1)} %get-tuple-element.90), slice={[0:2:1], [0:128:16], [0:2560:1]} | slice | bytes 163840 | tf_op jit(solution)/shard_map/slice | solution.py:58
  156.8 10.2 %slice.39 = bf16[2,8,2560]{1,2,0:T(8,128)(2,1)} slice(bf16[2,128,2560]{1,2,0:T(8,128)(2,1)S(1)} %get-tuple-element.91), slice={[0:2:1], [0:128:16], [0:2560:1]} | slice | bytes 163840 | tf_op jit(solution)/shard_map/slice | solution.py:58
  167.0 0.0 copy-done.1
  167.0 3.8 maximum_bitcast_fusion
  170.8 3.5 copy.27
  174.4 0.0 all-gather.2.cloned.1.call-update
  174.4 0.0 all-reduce.2.cloned.1.call-start
  174.4 0.0 copy-start.3
  174.4 0.0 copy-start.4
  174.5 0.6 copy.30
  175.1 1.6 copy.31
  176.8 0.1 copy.25
  176.9 0.1 reduce-window.8
  177.0 0.1 add_reduce_fusion
  177.1 11.7 %cosine_convert_fusion = (bf16[2560,256]{1,0:T(8,128)(2,1)S(1)}, bf16[2560,256]{1,0:T(8,128)(2,1)S(1)}) fusion(s32[256]{0:T(256)S(1)} %compare_select_fusion, s32[2560]{0:T(1024)S(1)} %iota_add_fusion), kind=kLoop, calls=%fused_computation.34 | loop fusion | flops 11141120 | bytes 2632704 | tf_op jit(solution)/shard_map/convert.9
  188.8 1.7 pad_maximum_fusion
  190.5 74.7 %all-gather.2.cloned.1.call-done = bf16[512,2,2,2560]{3,2,1,0:T(2,128)(2,1)} async-done(((bf16[8,2,2,2560]{3,2,1,0:T(2,128)(2,1)}), bf16[512,2,2,2560]{3,2,1,0:T(2,128)(2,1)}) %all-gather.2.cloned.1.call-update) | async-done | bytes 10485776 | tf_op jit(solution)/shard_map/all_gather | solution.py:63
  265.2 13.0 %reshape.97 = bf16[64,81920]{1,0:T(8,128)(2,1)} reshape(bf16[512,2,2,2560]{3,2,1,0:T(2,128)(2,1)} %all-gather.2.cloned.1.call-done) | data formatting | bytes 20971520 | tf_op jit(solution)/shard_map/reshape | solution.py:64
  278.2 13.8 %dot_general.11 = bf16[8,2,2,2560,64]{3,2,1,0,4:T(2,128)(2,1)} reshape(bf16[81920,64]{0,1:T(8,128)(2,1)} %bitcast.71) | data formatting | bytes 20971520 | tf_op jit(solution)/shard_map/dot_general | solution.py:65
  292.0 16.1 %fusion.8 = f32[4,8,2,2,2560]{4,0,3,2,1:T(4,128)} fusion(bf16[8,2,2,2560,64]{3,2,1,0,4:T(2,128)(2,1)} %dot_general.11, s32[64]{0:T(128)S(1)} %add_reduce_fusion, pred[64]{0:T(512)(128)(4,1)S(1)} %fusion.14), kind=kOutput, calls=%fused_computation.19 | convolution fusion | flops 41943552 | bytes 11796800 | tf_op jit(solution)/shard_map/dot_general | solution.py:65
  308.2 51.6 %while.10 = (s32[]{:T(128)}, f32[4,8,128,256]{3,2,1,0:T(8,128)}, f32[4,8,2,2,2560]{4,0,3,2,1:T(4,128)}, bf16[2,128,2560]{2,1,0:T(8,128)(2,1)S(1)}, bf16[2,128,25...) while((s32[]{:T(128)}, f32[4,8,128,256]{3,2,1,0:T(8,128)}, ...), condition=%wide.region_4.5_spmd, body=%wide.region_3.4_spmd.sunk | while | flops 2748841984 | bytes 53281388 | solution.py:88
  308.5 1.7 constant_dynamic-slice_fusion.3
  310.2 0.2 copy.51
  310.3 0.2 fusion.28
  310.6 0.7 bitcast_convert_fusion.5
  311.3 0.0 copy-start.2
  311.3 5.8 %add_convert_fusion.2 = (bf16[8,128,2560]{2,1,0:T(8,128)(2,1)S(1)}, bf16[8,128,2560]{2,1,0:T(8,128)(2,1)S(1)}) fusion(f32[128,2560]{1,0:T(8,128)S(1)} %get-tuple-element.145, f32[8,2560]{1,0:T(8,128)S(1)} %get-tuple-element.148, f32[128,2560]{1,0:T(8,128)S(1)} %get-tuple-element.149, f32[8,2560]{1,0:T(8,128)S(1)} %get-tuple-element.150, ...), kind=kLoop, calls=%fused_computation.5.clone.1 | loop fusion | flops 41943040 | bytes 16056320 | tf_op jit(solution)/shard_map/convert.7
  317.1 0.0 copy-done.2
  317.1 3.1 fusion.29
  320.2 1.1 constant_dynamic-update-slice_fusion.2
  321.3 1.7 constant_dynamic-slice_fusion.3
  323.0 0.2 copy.51
  323.1 0.2 fusion.28
  323.4 0.7 bitcast_convert_fusion.5
  324.1 5.8 %add_convert_fusion.2 = (bf16[8,128,2560]{2,1,0:T(8,128)(2,1)S(1)}, bf16[8,128,2560]{2,1,0:T(8,128)(2,1)S(1)}) fusion(f32[128,2560]{1,0:T(8,128)S(1)} %get-tuple-element.145, f32[8,2560]{1,0:T(8,128)S(1)} %get-tuple-element.148, f32[128,2560]{1,0:T(8,128)S(1)} %get-tuple-element.149, f32[8,2560]{1,0:T(8,128)S(1)} %get-tuple-element.150, ...), kind=kLoop, calls=%fused_computation.5.clone.1 | loop fusion | flops 41943040 | bytes 16056320 | tf_op jit(solution)/shard_map/convert.7
  329.9 3.1 fusion.29
  333.0 1.1 constant_dynamic-update-slice_fusion.2
  334.1 1.7 constant_dynamic-slice_fusion.3
  335.8 0.2 copy.51
  336.0 0.2 fusion.28
  336.2 0.7 bitcast_convert_fusion.5
  336.9 0.0 copy-start.2
  336.9 5.8 %add_convert_fusion.2 = (bf16[8,128,2560]{2,1,0:T(8,128)(2,1)S(1)}, bf16[8,128,2560]{2,1,0:T(8,128)(2,1)S(1)}) fusion(f32[128,2560]{1,0:T(8,128)S(1)} %get-tuple-element.145, f32[8,2560]{1,0:T(8,128)S(1)} %get-tuple-element.148, f32[128,2560]{1,0:T(8,128)S(1)} %get-tuple-element.149, f32[8,2560]{1,0:T(8,128)S(1)} %get-tuple-element.150, ...), kind=kLoop, calls=%fused_computation.5.clone.1 | loop fusion | flops 41943040 | bytes 16056320 | tf_op jit(solution)/shard_map/convert.7
  342.7 3.1 fusion.29
  345.8 1.1 constant_dynamic-update-slice_fusion.2
  346.9 1.7 constant_dynamic-slice_fusion.3
  348.6 0.2 copy.51
  348.8 0.2 fusion.28
  349.1 0.7 bitcast_convert_fusion.5
  349.8 5.8 %add_convert_fusion.2 = (bf16[8,128,2560]{2,1,0:T(8,128)(2,1)S(1)}, bf16[8,128,2560]{2,1,0:T(8,128)(2,1)S(1)}) fusion(f32[128,2560]{1,0:T(8,128)S(1)} %get-tuple-element.145, f32[8,2560]{1,0:T(8,128)S(1)} %get-tuple-element.148, f32[128,2560]{1,0:T(8,128)S(1)} %get-tuple-element.149, f32[8,2560]{1,0:T(8,128)S(1)} %get-tuple-element.150, ...), kind=kLoop, calls=%fused_computation.5.clone.1 | loop fusion | flops 41943040 | bytes 16056320 | tf_op jit(solution)/shard_map/convert.7
  355.6 3.1 fusion.29
  358.6 1.1 constant_dynamic-update-slice_fusion.2
  359.7 0.0 all-reduce.2.cloned.1.call-update
  359.8 94.6 %all-reduce.2.cloned.1.call-done = f32[4,8,128,256]{3,2,1,0:T(8,128)} async-done(((f32[4,8,128,256]{3,2,1,0:T(8,128)}), f32[4,8,128,256]{3,2,1,0:T(8,128)}) %all-reduce.2.cloned.1.call-update) | async-done | bytes 4194320 | tf_op jit(solution)/shard_map/psum | solution.py:89
  454.4 2.3 constant_dynamic-slice_fusion.1
  (20 shorter events, 0.2 us)
Async XLA Ops:
  6.5 258.7 %all-gather.2.cloned.1.call-start = ((), (), s32[]{:S(2)}) async-start(), calls=%async_computation | async-start | bytes 10649600 | tf_op jit(solution)/shard_map/all_gather | solution.py:63
  10.1 2.3 copy-start
  146.4 20.6 %copy-start.1 = (bf16[2,128,2560]{1,2,0:T(8,128)(2,1)}, bf16[2,128,2560]{1,2,0:T(8,128)(2,1)S(1)}, u32[]{:S(2)}) copy-start(bf16[2,128,2560]{1,2,0:T(8,128)(2,1)S(1)} %get-tuple-element.91) | copy-start | bytes 3932164
  174.4 280.0 %all-reduce.2.cloned.1.call-start = ((), (), s32[]{:S(2)}) async-start(), calls=%async_computation.1 | async-start | bytes 8388608 | tf_op jit(solution)/shard_map/psum | solution.py:89
  174.4 2.3 copy-start.3
  174.4 2.3 copy-start.4
  311.3 5.8 %copy-start.2 = (bf16[5120,256]{1,0:T(8,128)(2,1)S(1)}, bf16[5120,256]{1,0:T(8,128)(2,1)}, u32[]{:S(2)}) copy-start(bf16[5120,256]{1,0:T(8,128)(2,1)} %get-tuple-element.178) | copy-start | bytes 7864324 | tf_op jit(solution)/shard_map/while
  324.1 5.8 %copy-start.2 = (bf16[5120,256]{1,0:T(8,128)(2,1)S(1)}, bf16[5120,256]{1,0:T(8,128)(2,1)}, u32[]{:S(2)}) copy-start(bf16[5120,256]{1,0:T(8,128)(2,1)} %get-tuple-element.178) | copy-start | bytes 7864324 | tf_op jit(solution)/shard_map/while
  336.9 5.8 %copy-start.2 = (bf16[5120,256]{1,0:T(8,128)(2,1)S(1)}, bf16[5120,256]{1,0:T(8,128)(2,1)}, u32[]{:S(2)}) copy-start(bf16[5120,256]{1,0:T(8,128)(2,1)} %get-tuple-element.178) | copy-start | bytes 7864324 | tf_op jit(solution)/shard_map/while
  349.7 5.8 %copy-start.2 = (bf16[5120,256]{1,0:T(8,128)(2,1)S(1)}, bf16[5120,256]{1,0:T(8,128)(2,1)}, u32[]{:S(2)}) copy-start(bf16[5120,256]{1,0:T(8,128)(2,1)} %get-tuple-element.178) | copy-start | bytes 7864324 | tf_op jit(solution)/shard_map/while
Sparse Core Ops, SparseCore 0:
  174.5 90.6 all-gather.1
  359.9 94.4 all-reduce.1
where the time goes:
time: 467 us; the launch traced here: 464 us
  other arithmetic  178 us (38%)
  waiting for transfers between devices  169 us (36%)
  local copies, waits for them, and re-layouts  73.9 us (16%)
  matrix products  28.4 us (6%)
  between operations  14.1 us (3%)
    another operation x1, other arithmetic, whiten(): lax.reduce_window(amplitude, jnp.zeros((), amplitude.dtype), lax.add, win...  129 us
    psum x1, waiting for transfers between devices, shards(): summed_hours = lax.psum(partial_stacks, 'hour')  94.6 us
    all_gather x1, waiting for transfers between devices, shards(): gathered = lax.all_gather(local_sources, 'chan', axis=0, tiled=True)  74.7 us
    another operation x6, other arithmetic  34.9 us
    dot_general x1, matrix products, shards(): chosen = jnp.dot(onehot, flattened, preferred_element_type=jnp.float32)  16.1 us
    dot_general x1, local copies, waits for them, and re-layouts, shards(): chosen = jnp.dot(onehot, flattened, preferred_element_type=jnp.float32)  13.8 us
    reshape x1, local copies, waits for them, and re-layouts, shards(): flattened = gathered.reshape(block_count, -1)  13 us
    dot_general x4, matrix products, one_slot(): jnp.dot(cross, table_values, preferred_element_type=jnp.float32)  12.3 us
  transfers between devices with their start and end apart: 2, of which 2 were waited for; matrix products, arithmetic and copies ran while one was open for 3% of the time, Pallas kernels for 0%

commit v1 on v0

--- a/solution.py
+++ b/solution.py
@@ -60,7 +60,9 @@
     receiver = lax.axis_index("chan")
     onehot = slot_onehot(partner_lists, partner_counts, receiver).astype(jnp.bfloat16)
     slot_total = onehot.shape[0]
-    gathered = lax.all_gather(local_sources, "chan", axis=0, tiled=True)
+    gathered = jnp.concatenate(
+        lax.all_to_all(jnp.stack([local_sources] * lax.axis_size("chan")), "chan", 0, 0), axis=0
+    )
     flattened = gathered.reshape(block_count, -1)
     chosen = jnp.dot(onehot, flattened, preferred_element_type=jnp.float32)
     chosen = chosen.reshape(slot_total, VS, windows, 2, band_bins)

time: 467 us -> 624 us (1.34)
  waiting for transfers between devices: 169 us -> 309 us
  starting transfers between devices: 0.04 us -> 13.4 us
  local copies, waits for them, and re-layouts: 73.9 us -> 80.7 us
    all_to_all x0 -> x1, waiting for transfers between devices: none -> 215 us  [shards(): lax.all_to_all(jnp.stack([local_sources] * lax.axis_size('chan')), 'chan'...]
    all_gather x1 -> x0, waiting for transfers between devices: 74.7 us -> none  [shards(): gathered = lax.all_gather(local_sources, 'chan', axis=0, tiled=True)]
    another operation x0 -> x4, local copies, waits for them, and re-layouts: none -> 23.2 us  [the longest x1 13 us: shards(): flattened = gathered.reshape(block_count, -1)]
    all_to_all x0 -> x1, starting transfers between devices: none -> 13.3 us  [shards(): lax.all_to_all(jnp.stack([local_sources] * lax.axis_size('chan')), 'chan'...]
    reshape x1 -> x0, local copies, waits for them, and re-layouts: 13 us -> none  [shards(): flattened = gathered.reshape(block_count, -1)]
where the time goes in v1:
time: 624 us; the launch traced here: 621 us
  waiting for transfers between devices  309 us (50%)
  other arithmetic  175 us (28%)
  local copies, waits for them, and re-layouts  80.7 us (13%)
  matrix products  28.4 us (5%)
  between operations  14.1 us (2%)
  starting transfers between devices  13.4 us (2%)
    all_to_all x1, waiting for transfers between devices, shards(): lax.all_to_all(jnp.stack([local_sources] * lax.axis_size('chan')), 'chan'...  215 us
    another operation x1, other arithmetic, whiten(): lax.reduce_window(amplitude, jnp.zeros((), amplitude.dtype), lax.add, win...  130 us
    psum x1, waiting for transfers between devices, shards(): summed_hours = lax.psum(partial_stacks, 'hour')  94.8 us
    another operation x6, other arithmetic  34.9 us
    dot_general x1, matrix products, shards(): chosen = jnp.dot(onehot, flattened, preferred_element_type=jnp.float32)  16.1 us
    dot_general x1, local copies, waits for them, and re-layouts, shards(): chosen = jnp.dot(onehot, flattened, preferred_element_type=jnp.float32)  13.8 us
    all_to_all x1, starting transfers between devices, shards(): lax.all_to_all(jnp.stack([local_sources] * lax.axis_size('chan')), 'chan'...  13.3 us
    another operation x1, local copies, waits for them, and re-layouts, shards(): flattened = gathered.reshape(block_count, -1)  13 us
  transfers between devices with their start and end apart: 2, of which 2 were waited for; matrix products, arithmetic and copies ran while one was open for 3% of the time, Pallas kernels for 0%

profile of v1, /device:TPU:1, one launch (start us, length us, event | category | flops | bytes accessed | tf_op | source)
XLA Modules:
  0.0 621.3 jit_solution(1930923919226341317)
XLA Ops:
  6.5 3.2 copy.18
  9.8 0.3 convert_element_type.43
  10.1 0.0 copy-start
  10.1 2.3 copy-done
  12.4 0.8 add_sqrt_fusion
  13.3 129.9 %reduce_window.7 = f32[2,128,2560]{1,2,0:T(8,128)} reduce-window(f32[2,128,2560]{1,2,0:T(8,128)S(1)} %add_sqrt_fusion, f32[]{:T(128)} %constant.29.clone.1), window={size=1x1x129 pad=0_0x0_0x64_64}, to_apply=%region_2.0 | reduce-window | flops 83886080 | bytes 5242884 | tf_op jit(solution)/shard_map/reduce_window | solution.py:18
  143.2 4.0 divide_convert_fusion.1
  147.1 0.0 copy-start.1
  147.1 10.4 %slice.38 = bf16[2,8,2560]{1,2,0:T(8,128)(2,1)} slice(bf16[2,128,2560]{1,2,0:T(8,128)(2,1)S(1)} %get-tuple-element.84), slice={[0:2:1], [0:128:16], [0:2560:1]} | slice | bytes 163840 | tf_op jit(solution)/shard_map/slice | solution.py:58
  157.6 1.7 copy.19
  159.3 10.2 %slice.39 = bf16[2,8,2560]{1,2,0:T(8,128)(2,1)} slice(bf16[2,128,2560]{1,2,0:T(8,128)(2,1)S(1)} %get-tuple-element.85), slice={[0:2:1], [0:128:16], [0:2560:1]} | slice | bytes 163840 | tf_op jit(solution)/shard_map/slice | solution.py:58
  169.5 0.0 copy-done.1
  169.5 1.7 copy.20
  171.2 0.1 copy.21
  171.4 6.8 %stack.11 = bf16[64,8,2,2,2560]{4,3,2,1,0:T(2,128)(2,1)} broadcast(bf16[8,2,2,2560]{3,2,1,0:T(2,128)(2,1)S(1)} %copy.21), dimensions={1,2,3,4} | broadcast | bytes 10649600 | tf_op jit(solution)/shard_map/stack | solution.py:64
  178.2 13.3 %all-to-all-start = ((bf16[64,8,2,2,2560]{4,3,2,1,0:T(2,128)(2,1)}), bf16[64,8,2,2,2560]{4,3,2,1,0:T(2,128)(2,1)}, u32[]{:S(2)}, u32[]{:S(2)}) async-start(bf16[64,8,2,2,2560]{4,3,2,1,0:T(2,128)(2,1)} %stack.11), calls=%async_computation | async-start | bytes 20971520 | tf_op jit(solution)/shard_map/all_to_all | solution.py:64
  191.5 0.0 all-reduce.2.cloned.1.call-start
  191.6 0.0 copy-start.3
  191.6 0.0 copy-start.4
  191.6 0.6 copy.24
  192.2 1.6 copy.25
  193.9 0.1 copy.17
  194.0 0.1 reduce-window.8
  194.1 0.1 add_reduce_fusion
  194.2 11.7 %cosine_convert_fusion = (bf16[2560,256]{1,0:T(8,128)(2,1)S(1)}, bf16[2560,256]{1,0:T(8,128)(2,1)S(1)}) fusion(s32[256]{0:T(256)S(1)} %compare_select_fusion, s32[2560]{0:T(1024)S(1)} %iota_add_fusion), kind=kLoop, calls=%fused_computation.33 | loop fusion | flops 11141120 | bytes 2632704 | tf_op jit(solution)/shard_map/convert.9
  205.9 1.7 pad_maximum_fusion
  207.6 214.6 %all-to-all-done = bf16[64,8,2,2,2560]{4,3,2,1,0:T(2,128)(2,1)} async-done(((bf16[64,8,2,2,2560]{4,3,2,1,0:T(2,128)(2,1)}), bf16[64,8,2,2,2560]{4,3,2,1,0:T(2,128)(2,1)}, u32[]{:S(2)}, u32[]{:S(2)}) %all-to-all-start) | async-done | bytes 10485792 | tf_op jit(solution)/shard_map/all_to_all | solution.py:64
  422.3 13.0 %reshape_reshape.3 = bf16[64,81920]{1,0:T(8,128)(2,1)} reshape(bf16[64,8,2,2,2560]{4,3,2,1,0:T(2,128)(2,1)} %all-to-all-done) | data formatting | bytes 20971520 | tf_op jit(solution)/shard_map/reshape;reshape | solution.py:66
  435.2 13.8 %dot_general.11 = bf16[8,2,2,2560,64]{3,2,1,0,4:T(2,128)(2,1)} reshape(bf16[81920,64]{0,1:T(8,128)(2,1)} %bitcast.71) | data formatting | bytes 20971520 | tf_op jit(solution)/shard_map/dot_general | solution.py:67
  449.1 16.1 %fusion.8 = f32[4,8,2,2,2560]{4,0,3,2,1:T(4,128)} fusion(bf16[8,2,2,2560,64]{3,2,1,0,4:T(2,128)(2,1)} %dot_general.11, s32[64]{0:T(128)S(1)} %add_reduce_fusion, pred[64]{0:T(512)(128)(4,1)S(1)} %fusion.14), kind=kOutput, calls=%fused_computation.19 | convolution fusion | flops 41943552 | bytes 11796800 | tf_op jit(solution)/shard_map/dot_general | solution.py:67
  465.2 51.5 %while.10 = (s32[]{:T(128)}, f32[4,8,128,256]{3,2,1,0:T(8,128)}, f32[4,8,2,2,2560]{4,0,3,2,1:T(4,128)}, bf16[2,128,2560]{2,1,0:T(8,128)(2,1)S(1)}, bf16[2,128,25...) while((s32[]{:T(128)}, f32[4,8,128,256]{3,2,1,0:T(8,128)}, ...), condition=%wide.region_4.5_spmd, body=%wide.region_3.4_spmd.sunk | while | flops 2748841984 | bytes 53281388 | solution.py:90
  465.5 1.7 constant_dynamic-slice_fusion.3
  467.2 0.2 copy.45
  467.4 0.2 fusion.28
  467.7 0.7 bitcast_convert_fusion.5
  468.4 5.8 add_convert_fusion.2
  474.2 3.1 fusion.29
  477.3 1.1 constant_dynamic-update-slice_fusion.2
  478.4 1.7 constant_dynamic-slice_fusion.3
  480.0 0.2 copy.45
  480.2 0.2 fusion.28
  480.5 0.7 bitcast_convert_fusion.5
  481.2 5.8 add_convert_fusion.2
  487.0 3.1 fusion.29
  490.0 1.1 constant_dynamic-update-slice_fusion.2
  491.2 1.7 constant_dynamic-slice_fusion.3
  492.8 0.2 copy.45
  493.0 0.2 fusion.28
  493.3 0.7 bitcast_convert_fusion.5
  494.0 0.0 copy-start.2
  494.0 5.8 add_convert_fusion.2
  499.8 3.1 fusion.29
  502.9 1.1 constant_dynamic-update-slice_fusion.2
  504.0 1.7 constant_dynamic-slice_fusion.3
  505.6 0.2 copy.45
  505.8 0.2 fusion.28
  506.1 0.7 bitcast_convert_fusion.5
  506.8 5.8 add_convert_fusion.2
  512.6 0.0 copy-done.2
  512.6 3.1 fusion.29
  515.7 1.1 constant_dynamic-update-slice_fusion.2
  516.8 0.0 all-reduce.2.cloned.1.call-update
  516.8 94.8 %all-reduce.2.cloned.1.call-done = f32[4,8,128,256]{3,2,1,0:T(8,128)} async-done(((f32[4,8,128,256]{3,2,1,0:T(8,128)}), f32[4,8,128,256]{3,2,1,0:T(8,128)}) %all-reduce.2.cloned.1.call-update) | async-done | bytes 4194320 | tf_op jit(solution)/shard_map/psum | solution.py:91
  611.6 2.3 constant_dynamic-slice_fusion.1
  (22 shorter events, 0.2 us)
Async XLA Ops:
  10.1 2.3 copy-start
  147.1 22.4 %copy-start.1 = (bf16[2,128,2560]{1,2,0:T(8,128)(2,1)}, bf16[2,128,2560]{1,2,0:T(8,128)(2,1)S(1)}, u32[]{:S(2)}) copy-start(bf16[2,128,2560]{1,2,0:T(8,128)(2,1)S(1)} %get-tuple-element.85) | copy-start | bytes 3932164
  178.2 244.1 %all-to-all-start = ((bf16[64,8,2,2,2560]{4,3,2,1,0:T(2,128)(2,1)}), bf16[64,8,2,2,2560]{4,3,2,1,0:T(2,128)(2,1)}, u32[]{:S(2)}, u32[]{:S(2)}) async-start(bf16[64,8,2,2,2560]{4,3,2,1,0:T(2,128)(2,1)} %stack.11), calls=%async_computation | async-start | bytes 20971520 | tf_op jit(solution)/shard_map/all_to_all | solution.py:64
  191.5 420.1 %all-reduce.2.cloned.1.call-start = ((), (), s32[]{:S(2)}) async-start(), calls=%async_computation.1 | async-start | bytes 8388608 | tf_op jit(solution)/shard_map/psum | solution.py:91
  191.6 2.3 copy-start.3
  191.6 2.3 copy-start.4
  468.4 5.8 copy-start.2
  481.2 5.8 copy-start.2
  494.0 5.8 copy-start.2
  506.8 5.8 copy-start.2
Sparse Core Ops, SparseCore 0:
  516.9 94.6 all-reduce.1
